TPU v7x, 32 devices: a whole 2x2x4 slice. The times are simulated.
32 devices in a mesh: groups: 2 (over y), strip: 4 (over z), panel: 2 (over x), sub: 2 (over core).
Axes of the slice: x: 2, y: 2, z: 4, core: 2. Of those that a mesh axis runs over, the one named last changes fastest.
Arguments:
- start_block: float32 [64, 128, 256], P('groups', ('strip', 'sub'), 'panel'), parts along dimension 0, may hold values from -120 to 120, as said below
- edge_weights: float32 [16, 128, 256], P('groups', ('strip', 'sub'), 'panel'), parts along dimension 0, may hold values from 0 to 1, as said below
- mass: float32 [256, 256], P(('groups', 'strip', 'sub'), 'panel'), parts along dimension 0, may hold values from 0.5 to 2
- locked: bfloat16 [2048, 128, 256], P(('groups', 'panel'), ('strip', 'sub')), parts along dimension 0, may hold values from -4 to 4
Outputs:
- ortho: float32 [64, 128, 256], P('groups', ('strip', 'sub'), 'panel'), parts along dimension 0
- coupling: float32 [2048, 32], P(('groups', 'panel')), parts along dimension 0
- r_factor: float32 [64, 32], P('groups'), parts along dimension 0
There are 2 independent parts, one for each index of `groups`. A program takes and returns all parts, laid end to end along the dimension named above; each array names one. Nothing has to cross between parts.
Inputs may be any that keep to these rules, and one draw needn't show every extreme that they name: `start_block`: the sum of an entry's square over the block's vertices is positive for every vector. edge_weights[k + 4] at vertex (i, j) equals edge_weights[k] at vertex (i, j) - o_k for k = 0..3, and is zero where that vertex lies outside the grid; edge_weights[0..3] are positive everywhere.
All inputs are finite; a program needn't handle non-finite values.
Results may differ from a plain program's by a relative error of at most 0.003.
Values may be sent and summed in bfloat16 or wider, within the bound.
No kernel may reach another device: no remote copies, remote signals or barrier semaphores. Data moves between devices by JAX's collectives and lax.ppermute only.
A program may use at most 64 MiB of HBM per device.

v0:
```python
import math
import jax
import jax.numpy as jnp
from jax import lax
from jax.sharding import PartitionSpec as P

DEGREE = 6
CUT_LOW = 2
CUT_HIGH = 32
OFFSETS = ((0, 1), (1, 0), (1, 1), (1, -1), (0, -1), (-1, 0), (-1, -1), (-1, 1))


def with_halo(array, sides, width):
    for axis, dim in sides:
        devices, length = (lax.axis_size(axis), array.shape[dim])
        up = [(i, (i + 1) % devices) for i in range(devices - 1)]
        down = [(j, i) for i, j in up]
        last = lax.slice_in_dim(array, length - width, length, axis=dim)
        leading = lax.slice_in_dim(array, 0, width, axis=dim)
        before = lax.ppermute(last, axis, up)
        after = lax.ppermute(leading, axis, down)
        array = jnp.concatenate([before, array, after], axis=dim)
    return array


def apply_operator(vectors, edge_weights, scaling):
    scaled = scaling * vectors
    padded = with_halo(scaled, ((("strip", "sub"), 1), ("panel", 2)), 1)
    height = scaled.shape[1]
    across = scaled.shape[2]
    summed = jnp.zeros_like(scaled)
    for direction in range(8):
        step_row, step_col = OFFSETS[direction]
        beside = padded[
            :, 1 + step_row : 1 + step_row + height, 1 + step_col : 1 + step_col + across
        ]
        summed = summed + edge_weights[direction] * (scaled - beside)
    return scaling * summed


def chebyshev(start_block, edge_weights, scaling):
    centre = 0.5 * (CUT_HIGH + CUT_LOW)
    spread = 0.5 * (CUT_HIGH - CUT_LOW)
    previous = start_block
    current = (apply_operator(start_block, edge_weights, scaling) - centre * start_block) / spread
    for order_now in range(1, DEGREE):
        following = (
            2.0 * (apply_operator(current, edge_weights, scaling) - centre * current) / spread
            - previous
        )
        previous, current = (current, following)
    return current


def block_gram(flat_block):
    return jnp.dot(
        flat_block,
        flat_block.T,
        precision=lax.Precision.HIGHEST,
        preferred_element_type=jnp.float32,
    )


def on_device(start_block, edge_weights, mass, locked):
    scaling = 1.0 / jnp.sqrt(mass)
    filtered = chebyshev(start_block, edge_weights, scaling)
    block_count = filtered.shape[0]
    vertices = (
        filtered.shape[1]
        * filtered.shape[2]
        * lax.axis_size(("strip", "sub"))
        * lax.axis_size("panel")
    )
    identity_matrix = jnp.eye(block_count, dtype=jnp.float32)
    whole_rows = lax.all_gather(filtered, "panel", axis=2, tiled=True)
    flat_whole = whole_rows.reshape(block_count, -1)
    gram_matrix = (
        lax.psum(block_gram(flat_whole), ("strip", "sub")) / vertices + 1e-06 * identity_matrix
    )
    lower_factor = jnp.linalg.cholesky(gram_matrix)
    ortho_whole = lax.linalg.triangular_solve(
        lower_factor, flat_whole, left_side=True, lower=True
    ).reshape(whole_rows.shape)
    own_width = filtered.shape[2]
    ortho = lax.dynamic_slice_in_dim(ortho_whole, lax.axis_index("panel") * own_width, own_width, 2)
    ortho_half = ortho_whole.astype(jnp.bfloat16).reshape(block_count, -1)
    locked_flat = locked.reshape(locked.shape[0], -1)
    partial_coupling = jnp.einsum(
        "kn,bn->kb", locked_flat, ortho_half, preferred_element_type=jnp.float32
    )
    coupling = lax.psum(partial_coupling, ("strip", "sub")) / math.sqrt(float(vertices))
    return (ortho, coupling, jnp.transpose(lower_factor))


def solution(mesh):
    return jax.shard_map(
        on_device,
        mesh=mesh,
        in_specs=(
            P("groups", ("strip", "sub"), "panel"),
            P("groups", ("strip", "sub"), "panel"),
            P(("groups", "strip", "sub"), "panel"),
            P(("groups", "panel"), ("strip", "sub"), None),
        ),
        out_specs=(
            P("groups", ("strip", "sub"), "panel"),
            P(("groups", "panel"), None),
            P("groups", None),
        ),
        check_vma=False,
    )
```

profile of v0, /device:TPU:0, one launch (start us, length us, event | category | flops | bytes accessed | tf_op | source)
XLA Modules:
  0.0 241.3 jit_solution(13510634319213485302)
XLA Ops:
  9.0 2.4 collective-permute-start
  11.4 1.3 collective-permute-start.1
  12.7 4.0 %collective-permute-done.1 = f32[32,1,128]{2,0,1:T(8,128)S(1)} collective-permute-done((f32[32,1,128]{2,0,1:T(8,128)S(1)}, f32[32,1,128]{2,0,1:T(8,128)S(1)}, u32[]{:S(2)}, u32[]{:S(2)}) %collective-permute-start.1) | collective-permute-done | bytes 16416 | tf_op jit(solution)/shard_map/ppermute | solution.py:21
  16.8 1.3 collective-permute-start.2
  18.1 4.6 %collective-permute-start.3 = (f32[32,18,1]{2,0,1:T(8,128)S(1)}, f32[32,18,1]{2,0,1:T(8,128)S(1)}, u32[]{:S(2)}, u32[]{:S(2)}) collective-permute-start(f32[32,18,1]{2,0,1:T(8,128)S(1)} %get-tuple-element.41), channel_id=1, source_target_pairs={{0,2},{1,3},{4,6},{5,7},{8,10},{9,11},{12,14},{13,15},{16,18},{17,... | collective-permute-start | bytes 6920 | tf_op jit(solution)/shard_map/ppermute | solution.py:20
  23.5 3.5 %collective-permute-done.2 = f32[32,18,1]{2,0,1:T(8,128)S(1)} collective-permute-done((f32[32,18,1]{2,0,1:T(8,128)S(1)}, f32[32,18,1]{2,0,1:T(8,128)S(1)}, u32[]{:S(2)}, u32[]{:S(2)}) %collective-permute-start.2) | collective-permute-done | bytes 2336 | tf_op jit(solution)/shard_map/ppermute | solution.py:21
  27.0 1.8 collective-permute-done.3
  29.5 3.3 %collective-permute-start.4 = (f32[32,1,128]{2,0,1:T(8,128)S(1)}, f32[32,1,128]{2,0,1:T(8,128)S(1)}, u32[]{:S(2)}, u32[]{:S(2)}) collective-permute-start(f32[32,1,128]{2,0,1:T(8,128)S(1)} %get-tuple-element.51), channel_id=1, source_target_pairs={{0,1},{1,4},{4,5},{5,8},{8,9},{9,12},{12,13},{2,3},{3,6},{6,7},{7,... | collective-permute-start | bytes 49160 | tf_op jit(solution)/shard_map/ppermute | solution.py:20
  32.8 1.3 collective-permute-start.5
  34.1 3.3 %collective-permute-done.5 = f32[32,1,128]{2,0,1:T(8,128)S(1)} collective-permute-done((f32[32,1,128]{2,0,1:T(8,128)S(1)}, f32[32,1,128]{2,0,1:T(8,128)S(1)}, u32[]{:S(2)}, u32[]{:S(2)}) %collective-permute-start.5) | collective-permute-done | bytes 16416 | tf_op jit(solution)/shard_map/ppermute | solution.py:21
  37.6 1.3 collective-permute-start.6
  38.9 4.6 %collective-permute-start.7 = (f32[32,18,1]{2,0,1:T(8,128)S(1)}, f32[32,18,1]{2,0,1:T(8,128)S(1)}, u32[]{:S(2)}, u32[]{:S(2)}) collective-permute-start(f32[32,18,1]{2,0,1:T(8,128)S(1)} %get-tuple-element.37), channel_id=1, source_target_pairs={{0,2},{1,3},{4,6},{5,7},{8,10},{9,11},{12,14},{13,15},{16,18},{17,... | collective-permute-start | bytes 6920 | tf_op jit(solution)/shard_map/ppermute | solution.py:20
  43.5 4.2 %collective-permute-done.6 = f32[32,18,1]{2,0,1:T(8,128)S(1)} collective-permute-done((f32[32,18,1]{2,0,1:T(8,128)S(1)}, f32[32,18,1]{2,0,1:T(8,128)S(1)}, u32[]{:S(2)}, u32[]{:S(2)}) %collective-permute-start.6) | collective-permute-done | bytes 2336 | tf_op jit(solution)/shard_map/ppermute | solution.py:21
  47.7 1.8 collective-permute-done.7
  50.2 3.4 %collective-permute-start.8 = (f32[32,1,128]{2,0,1:T(8,128)S(1)}, f32[32,1,128]{2,0,1:T(8,128)S(1)}, u32[]{:S(2)}, u32[]{:S(2)}) collective-permute-start(f32[32,1,128]{2,0,1:T(8,128)S(1)} %get-tuple-element.49), channel_id=1, source_target_pairs={{0,1},{1,4},{4,5},{5,8},{8,9},{9,12},{12,13},{2,3},{3,6},{6,7},{7,... | collective-permute-start | bytes 49160 | tf_op jit(solution)/shard_map/ppermute | solution.py:20
  53.6 1.3 collective-permute-start.9
  54.9 3.2 %collective-permute-done.9 = f32[32,1,128]{2,0,1:T(8,128)S(1)} collective-permute-done((f32[32,1,128]{2,0,1:T(8,128)S(1)}, f32[32,1,128]{2,0,1:T(8,128)S(1)}, u32[]{:S(2)}, u32[]{:S(2)}) %collective-permute-start.9) | collective-permute-done | bytes 16416 | tf_op jit(solution)/shard_map/ppermute | solution.py:21
  58.3 1.3 collective-permute-start.10
  59.6 4.6 %collective-permute-start.11 = (f32[32,18,1]{2,0,1:T(8,128)S(1)}, f32[32,18,1]{2,0,1:T(8,128)S(1)}, u32[]{:S(2)}, u32[]{:S(2)}) collective-permute-start(f32[32,18,1]{2,0,1:T(8,128)S(1)} %get-tuple-element.33), channel_id=1, source_target_pairs={{0,2},{1,3},{4,6},{5,7},{8,10},{9,11},{12,14},{13,15},{16,18},{17,... | collective-permute-start | bytes 6920 | tf_op jit(solution)/shard_map/ppermute | solution.py:20
  64.2 4.2 %collective-permute-done.10 = f32[32,18,1]{2,0,1:T(8,128)S(1)} collective-permute-done((f32[32,18,1]{2,0,1:T(8,128)S(1)}, f32[32,18,1]{2,0,1:T(8,128)S(1)}, u32[]{:S(2)}, u32[]{:S(2)}) %collective-permute-start.10) | collective-permute-done | bytes 2336 | tf_op jit(solution)/shard_map/ppermute | solution.py:21
  68.4 1.8 collective-permute-done.11
  70.8 3.4 %collective-permute-start.12 = (f32[32,1,128]{2,0,1:T(8,128)S(1)}, f32[32,1,128]{2,0,1:T(8,128)S(1)}, u32[]{:S(2)}, u32[]{:S(2)}) collective-permute-start(f32[32,1,128]{2,0,1:T(8,128)S(1)} %get-tuple-element.47), channel_id=1, source_target_pairs={{0,1},{1,4},{4,5},{5,8},{8,9},{9,12},{12,13},{2,3},{3,6},{6,7},{7,... | collective-permute-start | bytes 49160 | tf_op jit(solution)/shard_map/ppermute | solution.py:20
  74.3 1.3 collective-permute-start.13
  75.6 3.5 %collective-permute-done.13 = f32[32,1,128]{2,0,1:T(8,128)S(1)} collective-permute-done((f32[32,1,128]{2,0,1:T(8,128)S(1)}, f32[32,1,128]{2,0,1:T(8,128)S(1)}, u32[]{:S(2)}, u32[]{:S(2)}) %collective-permute-start.13) | collective-permute-done | bytes 16416 | tf_op jit(solution)/shard_map/ppermute | solution.py:21
  79.2 1.3 collective-permute-start.14
  80.5 4.6 %collective-permute-start.15 = (f32[32,18,1]{2,0,1:T(8,128)S(1)}, f32[32,18,1]{2,0,1:T(8,128)S(1)}, u32[]{:S(2)}, u32[]{:S(2)}) collective-permute-start(f32[32,18,1]{2,0,1:T(8,128)S(1)} %get-tuple-element.29), channel_id=1, source_target_pairs={{0,2},{1,3},{4,6},{5,7},{8,10},{9,11},{12,14},{13,15},{16,18},{17,... | collective-permute-start | bytes 6920 | tf_op jit(solution)/shard_map/ppermute | solution.py:20
  85.1 4.2 %collective-permute-done.14 = f32[32,18,1]{2,0,1:T(8,128)S(1)} collective-permute-done((f32[32,18,1]{2,0,1:T(8,128)S(1)}, f32[32,18,1]{2,0,1:T(8,128)S(1)}, u32[]{:S(2)}, u32[]{:S(2)}) %collective-permute-start.14) | collective-permute-done | bytes 2336 | tf_op jit(solution)/shard_map/ppermute | solution.py:21
  89.3 1.8 collective-permute-done.15
  91.8 3.4 %collective-permute-start.16 = (f32[32,1,128]{2,0,1:T(8,128)S(1)}, f32[32,1,128]{2,0,1:T(8,128)S(1)}, u32[]{:S(2)}, u32[]{:S(2)}) collective-permute-start(f32[32,1,128]{2,0,1:T(8,128)S(1)} %get-tuple-element.45), channel_id=1, source_target_pairs={{0,1},{1,4},{4,5},{5,8},{8,9},{9,12},{12,13},{2,3},{3,6},{6,7},{7,... | collective-permute-start | bytes 49160 | tf_op jit(solution)/shard_map/ppermute | solution.py:20
  95.2 1.3 collective-permute-start.17
  96.5 2.7 %collective-permute-done.17 = f32[32,1,128]{2,0,1:T(8,128)S(1)} collective-permute-done((f32[32,1,128]{2,0,1:T(8,128)S(1)}, f32[32,1,128]{2,0,1:T(8,128)S(1)}, u32[]{:S(2)}, u32[]{:S(2)}) %collective-permute-start.17) | collective-permute-done | bytes 16416 | tf_op jit(solution)/shard_map/ppermute | solution.py:21
  99.4 1.3 collective-permute-start.18
  100.7 4.6 %collective-permute-start.19 = (f32[32,18,1]{2,0,1:T(8,128)S(1)}, f32[32,18,1]{2,0,1:T(8,128)S(1)}, u32[]{:S(2)}, u32[]{:S(2)}) collective-permute-start(f32[32,18,1]{2,0,1:T(8,128)S(1)} %get-tuple-element.25), channel_id=1, source_target_pairs={{0,2},{1,3},{4,6},{5,7},{8,10},{9,11},{12,14},{13,15},{16,18},{17,... | collective-permute-start | bytes 6920 | tf_op jit(solution)/shard_map/ppermute | solution.py:20
  105.3 4.2 %collective-permute-done.18 = f32[32,18,1]{2,0,1:T(8,128)S(1)} collective-permute-done((f32[32,18,1]{2,0,1:T(8,128)S(1)}, f32[32,18,1]{2,0,1:T(8,128)S(1)}, u32[]{:S(2)}, u32[]{:S(2)}) %collective-permute-start.18) | collective-permute-done | bytes 2336 | tf_op jit(solution)/shard_map/ppermute | solution.py:21
  109.5 1.8 collective-permute-done.19
  111.9 3.4 %collective-permute-start.20 = (f32[32,1,128]{2,0,1:T(8,128)S(1)}, f32[32,1,128]{2,0,1:T(8,128)S(1)}, u32[]{:S(2)}, u32[]{:S(2)}) collective-permute-start(f32[32,1,128]{2,0,1:T(8,128)S(1)} %get-tuple-element.43), channel_id=1, source_target_pairs={{0,1},{1,4},{4,5},{5,8},{8,9},{9,12},{12,13},{2,3},{3,6},{6,7},{7,... | collective-permute-start | bytes 49160 | tf_op jit(solution)/shard_map/ppermute | solution.py:20
  115.4 1.3 collective-permute-start.21
  116.7 1.8 collective-permute-done.21
  119.9 4.6 %collective-permute-start.23 = (f32[32,18,1]{2,0,1:T(8,128)S(1)}, f32[32,18,1]{2,0,1:T(8,128)S(1)}, u32[]{:S(2)}, u32[]{:S(2)}) collective-permute-start(f32[32,18,1]{2,0,1:T(8,128)S(1)} %get-tuple-element.21), channel_id=1, source_target_pairs={{0,2},{1,3},{4,6},{5,7},{8,10},{9,11},{12,14},{13,15},{16,18},{17,... | collective-permute-start | bytes 6920 | tf_op jit(solution)/shard_map/ppermute | solution.py:20
  124.5 4.3 %collective-permute-done.22 = f32[32,18,1]{2,0,1:T(8,128)S(1)} collective-permute-done((f32[32,18,1]{2,0,1:T(8,128)S(1)}, f32[32,18,1]{2,0,1:T(8,128)S(1)}, u32[]{:S(2)}, u32[]{:S(2)}) %collective-permute-start.22) | collective-permute-done | bytes 2336 | tf_op jit(solution)/shard_map/ppermute | solution.py:21
  128.8 1.8 collective-permute-done.23
  131.2 9.9 %all_gather.3 = f32[32,16,256]{2,0,1:T(8,128)S(1)} all-gather(f32[32,16,128]{2,0,1:T(8,128)S(1)} %fusion.13), channel_id=1, replica_groups=mesh['groups'=2,'strip'=4,'panel'=2,'sub'=2] {'panel'}, dimensions={2}, use_global_device_ids=true | all-gather | bytes 786432 | tf_op jit(solution)/shard_map/all_gather | solution.py:75
  141.7 26.0 %psum.14 = f32[32,32]{1,0:T(8,128)S(1)} all-reduce(f32[32,32]{1,0:T(8,128)S(1)} %convolution_bitcast_fusion), channel_id=1, replica_groups=mesh['groups'=2,'strip'=4,'panel'=2,'sub'=2] {'strip','sub'}, use_global_device_ids=true, to_apply=%region_0.0 | all-reduce | flops 1024 | bytes 8192 | tf_op jit(solution)/shard_map/psum | solution.py:78
  167.8 2.9 %cholesky.16 = f32[32,32]{1,0:T(8,128)S(1)} custom-call(f32[32,32]{1,0:T(8,128)S(1)} %fusion.134), custom_call_target="Cholesky" | custom-call | tf_op jit(solution)/shard_map/jit(cholesky)/cholesky | solution.py:80
  172.1 2.4 %custom-call.6 = f32[1,32,32]{1,2,0:T(8,128)S(1)} custom-call(f32[1,32,32]{2,1,0:T(8,128)S(1)} %get-tuple-element.64), custom_call_target="InvertDiagBlocksLowerTriangular" | custom-call | tf_op jit(solution)/shard_map/triangular_solve | solution.py:81
  175.2 5.2 %fusion.2 = f32[512,32]{0,1:T(8,128)} fusion(bf16[512,16,256]{2,1,0:T(8,128)(2,1)} %param.7, f32[32,16,256]{2,0,1:T(8,128)S(1)} %fusion.5), kind=kOutput, calls=%fused_computation.2 | convolution fusion | flops 134348800 | bytes 4784128 | tf_op jit(solution)/shard_map/kn,bn->kb/dot_general | solution.py:88
  181.9 51.1 %all-reduce.2.cloned.1.call-done = f32[512,32]{0,1:T(8,128)} async-done(((f32[512,32]{0,1:T(8,128)}), f32[512,32]{0,1:T(8,128)}) %all-reduce.2.cloned.1.call-update) | async-done | bytes 65552 | tf_op jit(solution)/shard_map/psum | solution.py:91
  233.0 1.5 broadcast_multiply_fusion.5
  (55 shorter events, 13.3 us)
Async XLA Ops:
  7.2 21.9 %copy-start = (f32[32,16,128]{2,1,0:T(8,128)S(1)}, f32[32,16,128]{2,1,0:T(8,128)}, u32[]{:S(2)}) copy-start(f32[32,16,128]{2,1,0:T(8,128)} %param.4) | copy-start | bytes 786436
  7.2 225.8 %all-reduce.2.cloned.1.call-start = ((), (), s32[]{:S(2)}) async-start(), calls=%async_computation | async-start | bytes 131072 | tf_op jit(solution)/shard_map/psum | solution.py:91
  9.0 3.7 %collective-permute-start = (f32[32,1,128]{2,0,1:T(8,128)S(1)}, f32[32,1,128]{2,0,1:T(8,128)S(1)}, u32[]{:S(2)}, u32[]{:S(2)}) collective-permute-start(f32[32,1,128]{2,0,1:T(8,128)S(1)} %get-tuple-element.53), channel_id=1, source_target_pairs={{0,1},{1,4},{4,5},{5,8},{8,9},{9,12},{12,13},{2,3},{3,6},{6,7},{7,... | collective-permute-start | bytes 49160 | tf_op jit(solution)/shard_map/ppermute | solution.py:20
  11.4 5.3 %collective-permute-start.1 = (f32[32,1,128]{2,0,1:T(8,128)S(1)}, f32[32,1,128]{2,0,1:T(8,128)S(1)}, u32[]{:S(2)}, u32[]{:S(2)}) collective-permute-start(f32[32,1,128]{2,0,1:T(8,128)S(1)} %get-tuple-element.54), channel_id=1, source_target_pairs={{1,0},{4,1},{5,4},{8,5},{9,8},{12,9},{13,12},{3,2},{6,3},{7,6},{10... | collective-permute-start | bytes 49160 | tf_op jit(solution)/shard_map/ppermute | solution.py:21
  16.8 10.2 %collective-permute-start.2 = (f32[32,18,1]{2,0,1:T(8,128)S(1)}, f32[32,18,1]{2,0,1:T(8,128)S(1)}, u32[]{:S(2)}, u32[]{:S(2)}) collective-permute-start(f32[32,18,1]{2,0,1:T(8,128)S(1)} %get-tuple-element.42), channel_id=1, source_target_pairs={{2,0},{3,1},{6,4},{7,5},{10,8},{11,9},{14,12},{15,13},{18,16},{19,... | collective-permute-start | bytes 6920 | tf_op jit(solution)/shard_map/ppermute | solution.py:21
  18.1 10.7 %collective-permute-start.3 = (f32[32,18,1]{2,0,1:T(8,128)S(1)}, f32[32,18,1]{2,0,1:T(8,128)S(1)}, u32[]{:S(2)}, u32[]{:S(2)}) collective-permute-start(f32[32,18,1]{2,0,1:T(8,128)S(1)} %get-tuple-element.41), channel_id=1, source_target_pairs={{0,2},{1,3},{4,6},{5,7},{8,10},{9,11},{12,14},{13,15},{16,18},{17,... | collective-permute-start | bytes 6920 | tf_op jit(solution)/shard_map/ppermute | solution.py:20
  29.5 4.6 %collective-permute-start.4 = (f32[32,1,128]{2,0,1:T(8,128)S(1)}, f32[32,1,128]{2,0,1:T(8,128)S(1)}, u32[]{:S(2)}, u32[]{:S(2)}) collective-permute-start(f32[32,1,128]{2,0,1:T(8,128)S(1)} %get-tuple-element.51), channel_id=1, source_target_pairs={{0,1},{1,4},{4,5},{5,8},{8,9},{9,12},{12,13},{2,3},{3,6},{6,7},{7,... | collective-permute-start | bytes 49160 | tf_op jit(solution)/shard_map/ppermute | solution.py:20
  32.8 4.6 %collective-permute-start.5 = (f32[32,1,128]{2,0,1:T(8,128)S(1)}, f32[32,1,128]{2,0,1:T(8,128)S(1)}, u32[]{:S(2)}, u32[]{:S(2)}) collective-permute-start(f32[32,1,128]{2,0,1:T(8,128)S(1)} %get-tuple-element.52), channel_id=1, source_target_pairs={{1,0},{4,1},{5,4},{8,5},{9,8},{12,9},{13,12},{3,2},{6,3},{7,6},{10... | collective-permute-start | bytes 49160 | tf_op jit(solution)/shard_map/ppermute | solution.py:21
  37.6 10.1 %collective-permute-start.6 = (f32[32,18,1]{2,0,1:T(8,128)S(1)}, f32[32,18,1]{2,0,1:T(8,128)S(1)}, u32[]{:S(2)}, u32[]{:S(2)}) collective-permute-start(f32[32,18,1]{2,0,1:T(8,128)S(1)} %get-tuple-element.38), channel_id=1, source_target_pairs={{2,0},{3,1},{6,4},{7,5},{10,8},{11,9},{14,12},{15,13},{18,16},{19,... | collective-permute-start | bytes 6920 | tf_op jit(solution)/shard_map/ppermute | solution.py:21
  38.9 10.6 %collective-permute-start.7 = (f32[32,18,1]{2,0,1:T(8,128)S(1)}, f32[32,18,1]{2,0,1:T(8,128)S(1)}, u32[]{:S(2)}, u32[]{:S(2)}) collective-permute-start(f32[32,18,1]{2,0,1:T(8,128)S(1)} %get-tuple-element.37), channel_id=1, source_target_pairs={{0,2},{1,3},{4,6},{5,7},{8,10},{9,11},{12,14},{13,15},{16,18},{17,... | collective-permute-start | bytes 6920 | tf_op jit(solution)/shard_map/ppermute | solution.py:20
  50.2 4.7 %collective-permute-start.8 = (f32[32,1,128]{2,0,1:T(8,128)S(1)}, f32[32,1,128]{2,0,1:T(8,128)S(1)}, u32[]{:S(2)}, u32[]{:S(2)}) collective-permute-start(f32[32,1,128]{2,0,1:T(8,128)S(1)} %get-tuple-element.49), channel_id=1, source_target_pairs={{0,1},{1,4},{4,5},{5,8},{8,9},{9,12},{12,13},{2,3},{3,6},{6,7},{7,... | collective-permute-start | bytes 49160 | tf_op jit(solution)/shard_map/ppermute | solution.py:20
  53.6 4.5 %collective-permute-start.9 = (f32[32,1,128]{2,0,1:T(8,128)S(1)}, f32[32,1,128]{2,0,1:T(8,128)S(1)}, u32[]{:S(2)}, u32[]{:S(2)}) collective-permute-start(f32[32,1,128]{2,0,1:T(8,128)S(1)} %get-tuple-element.50), channel_id=1, source_target_pairs={{1,0},{4,1},{5,4},{8,5},{9,8},{12,9},{13,12},{3,2},{6,3},{7,6},{10... | collective-permute-start | bytes 49160 | tf_op jit(solution)/shard_map/ppermute | solution.py:21
  58.3 10.1 %collective-permute-start.10 = (f32[32,18,1]{2,0,1:T(8,128)S(1)}, f32[32,18,1]{2,0,1:T(8,128)S(1)}, u32[]{:S(2)}, u32[]{:S(2)}) collective-permute-start(f32[32,18,1]{2,0,1:T(8,128)S(1)} %get-tuple-element.34), channel_id=1, source_target_pairs={{2,0},{3,1},{6,4},{7,5},{10,8},{11,9},{14,12},{15,13},{18,16},{19,... | collective-permute-start | bytes 6920 | tf_op jit(solution)/shard_map/ppermute | solution.py:21
  59.6 10.6 %collective-permute-start.11 = (f32[32,18,1]{2,0,1:T(8,128)S(1)}, f32[32,18,1]{2,0,1:T(8,128)S(1)}, u32[]{:S(2)}, u32[]{:S(2)}) collective-permute-start(f32[32,18,1]{2,0,1:T(8,128)S(1)} %get-tuple-element.33), channel_id=1, source_target_pairs={{0,2},{1,3},{4,6},{5,7},{8,10},{9,11},{12,14},{13,15},{16,18},{17,... | collective-permute-start | bytes 6920 | tf_op jit(solution)/shard_map/ppermute | solution.py:20
  70.8 4.7 %collective-permute-start.12 = (f32[32,1,128]{2,0,1:T(8,128)S(1)}, f32[32,1,128]{2,0,1:T(8,128)S(1)}, u32[]{:S(2)}, u32[]{:S(2)}) collective-permute-start(f32[32,1,128]{2,0,1:T(8,128)S(1)} %get-tuple-element.47), channel_id=1, source_target_pairs={{0,1},{1,4},{4,5},{5,8},{8,9},{9,12},{12,13},{2,3},{3,6},{6,7},{7,... | collective-permute-start | bytes 49160 | tf_op jit(solution)/shard_map/ppermute | solution.py:20
  74.3 4.8 %collective-permute-start.13 = (f32[32,1,128]{2,0,1:T(8,128)S(1)}, f32[32,1,128]{2,0,1:T(8,128)S(1)}, u32[]{:S(2)}, u32[]{:S(2)}) collective-permute-start(f32[32,1,128]{2,0,1:T(8,128)S(1)} %get-tuple-element.48), channel_id=1, source_target_pairs={{1,0},{4,1},{5,4},{8,5},{9,8},{12,9},{13,12},{3,2},{6,3},{7,6},{10... | collective-permute-start | bytes 49160 | tf_op jit(solution)/shard_map/ppermute | solution.py:21
  79.2 10.1 %collective-permute-start.14 = (f32[32,18,1]{2,0,1:T(8,128)S(1)}, f32[32,18,1]{2,0,1:T(8,128)S(1)}, u32[]{:S(2)}, u32[]{:S(2)}) collective-permute-start(f32[32,18,1]{2,0,1:T(8,128)S(1)} %get-tuple-element.30), channel_id=1, source_target_pairs={{2,0},{3,1},{6,4},{7,5},{10,8},{11,9},{14,12},{15,13},{18,16},{19,... | collective-permute-start | bytes 6920 | tf_op jit(solution)/shard_map/ppermute | solution.py:21
  80.5 10.6 %collective-permute-start.15 = (f32[32,18,1]{2,0,1:T(8,128)S(1)}, f32[32,18,1]{2,0,1:T(8,128)S(1)}, u32[]{:S(2)}, u32[]{:S(2)}) collective-permute-start(f32[32,18,1]{2,0,1:T(8,128)S(1)} %get-tuple-element.29), channel_id=1, source_target_pairs={{0,2},{1,3},{4,6},{5,7},{8,10},{9,11},{12,14},{13,15},{16,18},{17,... | collective-permute-start | bytes 6920 | tf_op jit(solution)/shard_map/ppermute | solution.py:20
  91.8 4.7 %collective-permute-start.16 = (f32[32,1,128]{2,0,1:T(8,128)S(1)}, f32[32,1,128]{2,0,1:T(8,128)S(1)}, u32[]{:S(2)}, u32[]{:S(2)}) collective-permute-start(f32[32,1,128]{2,0,1:T(8,128)S(1)} %get-tuple-element.45), channel_id=1, source_target_pairs={{0,1},{1,4},{4,5},{5,8},{8,9},{9,12},{12,13},{2,3},{3,6},{6,7},{7,... | collective-permute-start | bytes 49160 | tf_op jit(solution)/shard_map/ppermute | solution.py:20
  95.2 4.0 %collective-permute-start.17 = (f32[32,1,128]{2,0,1:T(8,128)S(1)}, f32[32,1,128]{2,0,1:T(8,128)S(1)}, u32[]{:S(2)}, u32[]{:S(2)}) collective-permute-start(f32[32,1,128]{2,0,1:T(8,128)S(1)} %get-tuple-element.46), channel_id=1, source_target_pairs={{1,0},{4,1},{5,4},{8,5},{9,8},{12,9},{13,12},{3,2},{6,3},{7,6},{10... | collective-permute-start | bytes 49160 | tf_op jit(solution)/shard_map/ppermute | solution.py:21
  99.4 10.1 %collective-permute-start.18 = (f32[32,18,1]{2,0,1:T(8,128)S(1)}, f32[32,18,1]{2,0,1:T(8,128)S(1)}, u32[]{:S(2)}, u32[]{:S(2)}) collective-permute-start(f32[32,18,1]{2,0,1:T(8,128)S(1)} %get-tuple-element.26), channel_id=1, source_target_pairs={{2,0},{3,1},{6,4},{7,5},{10,8},{11,9},{14,12},{15,13},{18,16},{19,... | collective-permute-start | bytes 6920 | tf_op jit(solution)/shard_map/ppermute | solution.py:21
  100.7 10.6 %collective-permute-start.19 = (f32[32,18,1]{2,0,1:T(8,128)S(1)}, f32[32,18,1]{2,0,1:T(8,128)S(1)}, u32[]{:S(2)}, u32[]{:S(2)}) collective-permute-start(f32[32,18,1]{2,0,1:T(8,128)S(1)} %get-tuple-element.25), channel_id=1, source_target_pairs={{0,2},{1,3},{4,6},{5,7},{8,10},{9,11},{12,14},{13,15},{16,18},{17,... | collective-permute-start | bytes 6920 | tf_op jit(solution)/shard_map/ppermute | solution.py:20
  111.9 4.7 %collective-permute-start.20 = (f32[32,1,128]{2,0,1:T(8,128)S(1)}, f32[32,1,128]{2,0,1:T(8,128)S(1)}, u32[]{:S(2)}, u32[]{:S(2)}) collective-permute-start(f32[32,1,128]{2,0,1:T(8,128)S(1)} %get-tuple-element.43), channel_id=1, source_target_pairs={{0,1},{1,4},{4,5},{5,8},{8,9},{9,12},{12,13},{2,3},{3,6},{6,7},{7,... | collective-permute-start | bytes 49160 | tf_op jit(solution)/shard_map/ppermute | solution.py:20
  115.4 3.1 %collective-permute-start.21 = (f32[32,1,128]{2,0,1:T(8,128)S(1)}, f32[32,1,128]{2,0,1:T(8,128)S(1)}, u32[]{:S(2)}, u32[]{:S(2)}) collective-permute-start(f32[32,1,128]{2,0,1:T(8,128)S(1)} %get-tuple-element.44), channel_id=1, source_target_pairs={{1,0},{4,1},{5,4},{8,5},{9,8},{12,9},{13,12},{3,2},{6,3},{7,6},{10... | collective-permute-start | bytes 49160 | tf_op jit(solution)/shard_map/ppermute | solution.py:21
  118.6 10.1 %collective-permute-start.22 = (f32[32,18,1]{2,0,1:T(8,128)S(1)}, f32[32,18,1]{2,0,1:T(8,128)S(1)}, u32[]{:S(2)}, u32[]{:S(2)}) collective-permute-start(f32[32,18,1]{2,0,1:T(8,128)S(1)} %get-tuple-element.22), channel_id=1, source_target_pairs={{2,0},{3,1},{6,4},{7,5},{10,8},{11,9},{14,12},{15,13},{18,16},{19,... | collective-permute-start | bytes 6920 | tf_op jit(solution)/shard_map/ppermute | solution.py:21
  119.9 10.6 %collective-permute-start.23 = (f32[32,18,1]{2,0,1:T(8,128)S(1)}, f32[32,18,1]{2,0,1:T(8,128)S(1)}, u32[]{:S(2)}, u32[]{:S(2)}) collective-permute-start(f32[32,18,1]{2,0,1:T(8,128)S(1)} %get-tuple-element.21), channel_id=1, source_target_pairs={{0,2},{1,3},{4,6},{5,7},{8,10},{9,11},{12,14},{13,15},{16,18},{17,... | collective-permute-start | bytes 6920 | tf_op jit(solution)/shard_map/ppermute | solution.py:20
Sparse Core Ops, SparseCore 0:
  180.5 52.4 all-reduce.1
where the time goes:
time: 242 us; the launch traced here: 241 us
  waiting for transfers between devices  105 us (43%)
  starting transfers between devices  62.3 us (26%)
  blocking collectives  35.9 us (15%)
  between operations  14.5 us (6%)
  other arithmetic  14.2 us (6%)
  matrix products  6.4 us (3%)
  local copies, waits for them, and re-layouts  3.36 us (1%)
    psum x1, waiting for transfers between devices, on_device(): lax.psum(partial_coupling, ('strip', 'sub')) / math.sqrt(float(vertices))  51.1 us
    ppermute x12, starting transfers between devices, with_halo(): before = lax.ppermute(last, axis, up)  46.8 us
    ppermute x12, waiting for transfers between devices, with_halo(): after = lax.ppermute(leading, axis, down)  42.9 us
    psum x1, blocking collectives, on_device(): lax.psum(block_gram(flat_whole), ('strip', 'sub')) / vertices  26 us
    ppermute x12, starting transfers between devices, with_halo(): after = lax.ppermute(leading, axis, down)  15.5 us
    ppermute x12, waiting for transfers between devices, with_halo(): before = lax.ppermute(last, axis, up)  10.7 us
    all_gather x1, blocking collectives, on_device(): whole_rows = lax.all_gather(filtered, 'panel', axis=2, tiled=True)  9.93 us
    dot_general x1, matrix products, on_device(): jnp.einsum('kn,bn->kb', locked_flat, ortho_half, preferred_element_type=j...  5.19 us
  transfers between devices with their start and end apart: 25, of which 19 were waited for; matrix products, arithmetic and copies ran while one was open for 1% of the time, Pallas kernels for 0%

commit v1 on v0

--- a/solution.py
+++ b/solution.py
@@ -88,7 +88,9 @@
     partial_coupling = jnp.einsum(
         "kn,bn->kb", locked_flat, ortho_half, preferred_element_type=jnp.float32
     )
-    coupling = lax.psum(partial_coupling, ("strip", "sub")) / math.sqrt(float(vertices))
+    coupling = jnp.sum(lax.all_gather(partial_coupling, ("strip", "sub")), axis=0) / math.sqrt(
+        float(vertices)
+    )
     return (ortho, coupling, jnp.transpose(lower_factor))
 
 

time: 242 us -> 192 us (0.79)
  waiting for transfers between devices: 105 us -> 53.6 us
  blocking collectives: 35.9 us -> 50.9 us
  between operations: 14.5 us -> 1.11 us
    psum x1 -> x0, waiting for transfers between devices: 51.1 us -> none  [on_device(): lax.psum(partial_coupling, ('strip', 'sub')) / math.sqrt(float(vertices))]
    all_gather x0 -> x1, blocking collectives: none -> 15 us  [on_device(): lax.all_gather(partial_coupling, ('strip', 'sub'))]
  transfers between devices with their start and end apart: 25 -> 24, of which waited for: 19 -> 18; matrix products, arithmetic and copies ran while one was open for 1% -> 0% of each run, Pallas kernels for 0% -> 0%
where the time goes in v1:
time: 192 us; the launch traced here: 191 us
  starting transfers between devices  62.3 us (32%)
  waiting for transfers between devices  53.6 us (28%)
  blocking collectives  50.9 us (27%)
  other arithmetic  13.4 us (7%)
  matrix products  5.77 us (3%)
  local copies, waits for them, and re-layouts  3.66 us (2%)
    ppermute x12, starting transfers between devices, with_halo(): before = lax.ppermute(last, axis, up)  46.8 us
    ppermute x12, waiting for transfers between devices, with_halo(): after = lax.ppermute(leading, axis, down)  42.9 us
    psum x1, blocking collectives, on_device(): lax.psum(block_gram(flat_whole), ('strip', 'sub')) / vertices  26 us
    ppermute x12, starting transfers between devices, with_halo(): after = lax.ppermute(leading, axis, down)  15.5 us
    all_gather x1, blocking collectives, on_device(): lax.all_gather(partial_coupling, ('strip', 'sub'))  15 us
    ppermute x12, waiting for transfers between devices, with_halo(): before = lax.ppermute(last, axis, up)  10.7 us
    all_gather x1, blocking collectives, on_device(): whole_rows = lax.all_gather(filtered, 'panel', axis=2, tiled=True)  9.93 us
    dot_general x1, matrix products, on_device(): jnp.einsum('kn,bn->kb', locked_flat, ortho_half, preferred_element_type=j...  4.57 us
  transfers between devices with their start and end apart: 24, of which 18 were waited for; matrix products, arithmetic and copies ran while one was open for 0% of the time, Pallas kernels for 0%

profile of v1, /device:TPU:0, one launch (start us, length us, event | category | flops | bytes accessed | tf_op | source)
XLA Modules:
  0.0 190.7 jit_solution(10894134431964838497)
XLA Ops:
  2.4 2.4 %collective-permute-start = (f32[32,1,128]{2,0,1:T(8,128)S(1)}, f32[32,1,128]{2,0,1:T(8,128)S(1)}, u32[]{:S(2)}, u32[]{:S(2)}) collective-permute-start(f32[32,1,128]{2,0,1:T(8,128)S(1)} %get-tuple-element.53), channel_id=1, source_target_pairs={{0,1},{1,4},{4,5},{5,8},{8,9},{9,12},{12,13},{2,3},{3,6},{6,7},{7,... | collective-permute-start | bytes 49160 | tf_op jit(solution)/shard_map/ppermute | solution.py:20
  4.8 1.3 collective-permute-start.1
  6.1 4.0 %collective-permute-done.1 = f32[32,1,128]{2,0,1:T(8,128)S(1)} collective-permute-done((f32[32,1,128]{2,0,1:T(8,128)S(1)}, f32[32,1,128]{2,0,1:T(8,128)S(1)}, u32[]{:S(2)}, u32[]{:S(2)}) %collective-permute-start.1) | collective-permute-done | bytes 16416 | tf_op jit(solution)/shard_map/ppermute | solution.py:21
  10.3 1.3 collective-permute-start.2
  11.6 4.6 %collective-permute-start.3 = (f32[32,18,1]{2,0,1:T(8,128)S(1)}, f32[32,18,1]{2,0,1:T(8,128)S(1)}, u32[]{:S(2)}, u32[]{:S(2)}) collective-permute-start(f32[32,18,1]{2,0,1:T(8,128)S(1)} %get-tuple-element.41), channel_id=1, source_target_pairs={{0,2},{1,3},{4,6},{5,7},{8,10},{9,11},{12,14},{13,15},{16,18},{17,... | collective-permute-start | bytes 6920 | tf_op jit(solution)/shard_map/ppermute | solution.py:20
  17.0 3.5 %collective-permute-done.2 = f32[32,18,1]{2,0,1:T(8,128)S(1)} collective-permute-done((f32[32,18,1]{2,0,1:T(8,128)S(1)}, f32[32,18,1]{2,0,1:T(8,128)S(1)}, u32[]{:S(2)}, u32[]{:S(2)}) %collective-permute-start.2) | collective-permute-done | bytes 2336 | tf_op jit(solution)/shard_map/ppermute | solution.py:21
  20.5 1.8 collective-permute-done.3
  22.9 3.3 %collective-permute-start.4 = (f32[32,1,128]{2,0,1:T(8,128)S(1)}, f32[32,1,128]{2,0,1:T(8,128)S(1)}, u32[]{:S(2)}, u32[]{:S(2)}) collective-permute-start(f32[32,1,128]{2,0,1:T(8,128)S(1)} %get-tuple-element.51), channel_id=1, source_target_pairs={{0,1},{1,4},{4,5},{5,8},{8,9},{9,12},{12,13},{2,3},{3,6},{6,7},{7,... | collective-permute-start | bytes 49160 | tf_op jit(solution)/shard_map/ppermute | solution.py:20
  26.2 1.3 collective-permute-start.5
  27.5 3.3 %collective-permute-done.5 = f32[32,1,128]{2,0,1:T(8,128)S(1)} collective-permute-done((f32[32,1,128]{2,0,1:T(8,128)S(1)}, f32[32,1,128]{2,0,1:T(8,128)S(1)}, u32[]{:S(2)}, u32[]{:S(2)}) %collective-permute-start.5) | collective-permute-done | bytes 16416 | tf_op jit(solution)/shard_map/ppermute | solution.py:21
  31.0 1.3 collective-permute-start.6
  32.3 4.6 %collective-permute-start.7 = (f32[32,18,1]{2,0,1:T(8,128)S(1)}, f32[32,18,1]{2,0,1:T(8,128)S(1)}, u32[]{:S(2)}, u32[]{:S(2)}) collective-permute-start(f32[32,18,1]{2,0,1:T(8,128)S(1)} %get-tuple-element.37), channel_id=1, source_target_pairs={{0,2},{1,3},{4,6},{5,7},{8,10},{9,11},{12,14},{13,15},{16,18},{17,... | collective-permute-start | bytes 6920 | tf_op jit(solution)/shard_map/ppermute | solution.py:20
  36.9 4.2 %collective-permute-done.6 = f32[32,18,1]{2,0,1:T(8,128)S(1)} collective-permute-done((f32[32,18,1]{2,0,1:T(8,128)S(1)}, f32[32,18,1]{2,0,1:T(8,128)S(1)}, u32[]{:S(2)}, u32[]{:S(2)}) %collective-permute-start.6) | collective-permute-done | bytes 2336 | tf_op jit(solution)/shard_map/ppermute | solution.py:21
  41.1 1.8 collective-permute-done.7
  43.6 3.4 %collective-permute-start.8 = (f32[32,1,128]{2,0,1:T(8,128)S(1)}, f32[32,1,128]{2,0,1:T(8,128)S(1)}, u32[]{:S(2)}, u32[]{:S(2)}) collective-permute-start(f32[32,1,128]{2,0,1:T(8,128)S(1)} %get-tuple-element.49), channel_id=1, source_target_pairs={{0,1},{1,4},{4,5},{5,8},{8,9},{9,12},{12,13},{2,3},{3,6},{6,7},{7,... | collective-permute-start | bytes 49160 | tf_op jit(solution)/shard_map/ppermute | solution.py:20
  47.0 1.3 collective-permute-start.9
  48.3 3.2 %collective-permute-done.9 = f32[32,1,128]{2,0,1:T(8,128)S(1)} collective-permute-done((f32[32,1,128]{2,0,1:T(8,128)S(1)}, f32[32,1,128]{2,0,1:T(8,128)S(1)}, u32[]{:S(2)}, u32[]{:S(2)}) %collective-permute-start.9) | collective-permute-done | bytes 16416 | tf_op jit(solution)/shard_map/ppermute | solution.py:21
  51.7 1.3 collective-permute-start.10
  53.0 4.6 %collective-permute-start.11 = (f32[32,18,1]{2,0,1:T(8,128)S(1)}, f32[32,18,1]{2,0,1:T(8,128)S(1)}, u32[]{:S(2)}, u32[]{:S(2)}) collective-permute-start(f32[32,18,1]{2,0,1:T(8,128)S(1)} %get-tuple-element.33), channel_id=1, source_target_pairs={{0,2},{1,3},{4,6},{5,7},{8,10},{9,11},{12,14},{13,15},{16,18},{17,... | collective-permute-start | bytes 6920 | tf_op jit(solution)/shard_map/ppermute | solution.py:20
  57.6 4.2 %collective-permute-done.10 = f32[32,18,1]{2,0,1:T(8,128)S(1)} collective-permute-done((f32[32,18,1]{2,0,1:T(8,128)S(1)}, f32[32,18,1]{2,0,1:T(8,128)S(1)}, u32[]{:S(2)}, u32[]{:S(2)}) %collective-permute-start.10) | collective-permute-done | bytes 2336 | tf_op jit(solution)/shard_map/ppermute | solution.py:21
  61.8 1.8 collective-permute-done.11
  64.2 3.4 %collective-permute-start.12 = (f32[32,1,128]{2,0,1:T(8,128)S(1)}, f32[32,1,128]{2,0,1:T(8,128)S(1)}, u32[]{:S(2)}, u32[]{:S(2)}) collective-permute-start(f32[32,1,128]{2,0,1:T(8,128)S(1)} %get-tuple-element.47), channel_id=1, source_target_pairs={{0,1},{1,4},{4,5},{5,8},{8,9},{9,12},{12,13},{2,3},{3,6},{6,7},{7,... | collective-permute-start | bytes 49160 | tf_op jit(solution)/shard_map/ppermute | solution.py:20
  67.7 1.3 collective-permute-start.13
  69.0 3.5 %collective-permute-done.13 = f32[32,1,128]{2,0,1:T(8,128)S(1)} collective-permute-done((f32[32,1,128]{2,0,1:T(8,128)S(1)}, f32[32,1,128]{2,0,1:T(8,128)S(1)}, u32[]{:S(2)}, u32[]{:S(2)}) %collective-permute-start.13) | collective-permute-done | bytes 16416 | tf_op jit(solution)/shard_map/ppermute | solution.py:21
  72.6 1.3 collective-permute-start.14
  73.9 4.6 %collective-permute-start.15 = (f32[32,18,1]{2,0,1:T(8,128)S(1)}, f32[32,18,1]{2,0,1:T(8,128)S(1)}, u32[]{:S(2)}, u32[]{:S(2)}) collective-permute-start(f32[32,18,1]{2,0,1:T(8,128)S(1)} %get-tuple-element.29), channel_id=1, source_target_pairs={{0,2},{1,3},{4,6},{5,7},{8,10},{9,11},{12,14},{13,15},{16,18},{17,... | collective-permute-start | bytes 6920 | tf_op jit(solution)/shard_map/ppermute | solution.py:20
  78.5 4.2 %collective-permute-done.14 = f32[32,18,1]{2,0,1:T(8,128)S(1)} collective-permute-done((f32[32,18,1]{2,0,1:T(8,128)S(1)}, f32[32,18,1]{2,0,1:T(8,128)S(1)}, u32[]{:S(2)}, u32[]{:S(2)}) %collective-permute-start.14) | collective-permute-done | bytes 2336 | tf_op jit(solution)/shard_map/ppermute | solution.py:21
  82.7 1.8 collective-permute-done.15
  85.1 3.4 %collective-permute-start.16 = (f32[32,1,128]{2,0,1:T(8,128)S(1)}, f32[32,1,128]{2,0,1:T(8,128)S(1)}, u32[]{:S(2)}, u32[]{:S(2)}) collective-permute-start(f32[32,1,128]{2,0,1:T(8,128)S(1)} %get-tuple-element.45), channel_id=1, source_target_pairs={{0,1},{1,4},{4,5},{5,8},{8,9},{9,12},{12,13},{2,3},{3,6},{6,7},{7,... | collective-permute-start | bytes 49160 | tf_op jit(solution)/shard_map/ppermute | solution.py:20
  88.6 1.3 collective-permute-start.17
  89.9 2.7 %collective-permute-done.17 = f32[32,1,128]{2,0,1:T(8,128)S(1)} collective-permute-done((f32[32,1,128]{2,0,1:T(8,128)S(1)}, f32[32,1,128]{2,0,1:T(8,128)S(1)}, u32[]{:S(2)}, u32[]{:S(2)}) %collective-permute-start.17) | collective-permute-done | bytes 16416 | tf_op jit(solution)/shard_map/ppermute | solution.py:21
  92.8 1.3 collective-permute-start.18
  94.1 4.6 %collective-permute-start.19 = (f32[32,18,1]{2,0,1:T(8,128)S(1)}, f32[32,18,1]{2,0,1:T(8,128)S(1)}, u32[]{:S(2)}, u32[]{:S(2)}) collective-permute-start(f32[32,18,1]{2,0,1:T(8,128)S(1)} %get-tuple-element.25), channel_id=1, source_target_pairs={{0,2},{1,3},{4,6},{5,7},{8,10},{9,11},{12,14},{13,15},{16,18},{17,... | collective-permute-start | bytes 6920 | tf_op jit(solution)/shard_map/ppermute | solution.py:20
  98.7 4.2 %collective-permute-done.18 = f32[32,18,1]{2,0,1:T(8,128)S(1)} collective-permute-done((f32[32,18,1]{2,0,1:T(8,128)S(1)}, f32[32,18,1]{2,0,1:T(8,128)S(1)}, u32[]{:S(2)}, u32[]{:S(2)}) %collective-permute-start.18) | collective-permute-done | bytes 2336 | tf_op jit(solution)/shard_map/ppermute | solution.py:21
  102.9 1.8 collective-permute-done.19
  105.3 3.4 %collective-permute-start.20 = (f32[32,1,128]{2,0,1:T(8,128)S(1)}, f32[32,1,128]{2,0,1:T(8,128)S(1)}, u32[]{:S(2)}, u32[]{:S(2)}) collective-permute-start(f32[32,1,128]{2,0,1:T(8,128)S(1)} %get-tuple-element.43), channel_id=1, source_target_pairs={{0,1},{1,4},{4,5},{5,8},{8,9},{9,12},{12,13},{2,3},{3,6},{6,7},{7,... | collective-permute-start | bytes 49160 | tf_op jit(solution)/shard_map/ppermute | solution.py:20
  108.7 1.3 collective-permute-start.21
  110.0 1.8 collective-permute-done.21
  112.0 1.3 collective-permute-start.22
  113.3 4.6 %collective-permute-start.23 = (f32[32,18,1]{2,0,1:T(8,128)S(1)}, f32[32,18,1]{2,0,1:T(8,128)S(1)}, u32[]{:S(2)}, u32[]{:S(2)}) collective-permute-start(f32[32,18,1]{2,0,1:T(8,128)S(1)} %get-tuple-element.21), channel_id=1, source_target_pairs={{0,2},{1,3},{4,6},{5,7},{8,10},{9,11},{12,14},{13,15},{16,18},{17,... | collective-permute-start | bytes 6920 | tf_op jit(solution)/shard_map/ppermute | solution.py:20
  117.9 4.3 %collective-permute-done.22 = f32[32,18,1]{2,0,1:T(8,128)S(1)} collective-permute-done((f32[32,18,1]{2,0,1:T(8,128)S(1)}, f32[32,18,1]{2,0,1:T(8,128)S(1)}, u32[]{:S(2)}, u32[]{:S(2)}) %collective-permute-start.22) | collective-permute-done | bytes 2336 | tf_op jit(solution)/shard_map/ppermute | solution.py:21
  122.1 1.8 collective-permute-done.23
  124.6 9.9 %all_gather.9 = f32[32,16,256]{2,0,1:T(8,128)S(1)} all-gather(f32[32,16,128]{2,0,1:T(8,128)S(1)} %fusion.13), channel_id=1, replica_groups=mesh['groups'=2,'strip'=4,'panel'=2,'sub'=2] {'panel'}, dimensions={2}, use_global_device_ids=true | all-gather | bytes 786432 | tf_op jit(solution)/shard_map/all_gather | solution.py:75
  135.1 26.0 %psum.7 = f32[32,32]{1,0:T(8,128)S(1)} all-reduce(f32[32,32]{1,0:T(8,128)S(1)} %convolution_bitcast_fusion), channel_id=1, replica_groups=mesh['groups'=2,'strip'=4,'panel'=2,'sub'=2] {'strip','sub'}, use_global_device_ids=true, to_apply=%region_0.0 | all-reduce | flops 1024 | bytes 8192 | tf_op jit(solution)/shard_map/psum | solution.py:78
  161.1 2.9 %cholesky.16 = f32[32,32]{1,0:T(8,128)S(1)} custom-call(f32[32,32]{1,0:T(8,128)S(1)} %fusion.134), custom_call_target="Cholesky" | custom-call | tf_op jit(solution)/shard_map/jit(cholesky)/cholesky | solution.py:80
  165.4 2.4 %custom-call.6 = f32[1,32,32]{1,2,0:T(8,128)S(1)} custom-call(f32[1,32,32]{2,1,0:T(8,128)S(1)} %get-tuple-element.64), custom_call_target="InvertDiagBlocksLowerTriangular" | custom-call | tf_op jit(solution)/shard_map/triangular_solve | solution.py:81
  168.5 4.6 %fusion.2 = f32[512,32]{0,1:T(8,128)S(1)} fusion(bf16[512,16,256]{2,1,0:T(8,128)(2,1)} %param.7, f32[32,16,256]{2,0,1:T(8,128)S(1)} %fusion.5), kind=kOutput, calls=%fused_computation.2 | convolution fusion | flops 134348800 | bytes 4784128 | tf_op jit(solution)/shard_map/kn,bn->kb/dot_general | solution.py:88
  173.1 15.0 %all-gather = f32[4096,32]{0,1:T(8,128)S(1)} all-gather(f32[512,32]{0,1:T(8,128)S(1)} %fusion.2), channel_id=2, replica_groups=mesh['groups'=2,'strip'=4,'panel'=2,'sub'=2] {'strip','sub'}, dimensions={0}, use_global_device_ids=true | all-gather | bytes 589824 | tf_op jit(solution)/shard_map/all_gather | solution.py:91
  (55 shorter events, 12.9 us)
Async XLA Ops:
  0.6 21.8 %copy-start = (f32[32,16,128]{2,1,0:T(8,128)S(1)}, f32[32,16,128]{2,1,0:T(8,128)}, u32[]{:S(2)}) copy-start(f32[32,16,128]{2,1,0:T(8,128)} %param.4) | copy-start | bytes 786436
  2.4 3.7 %collective-permute-start = (f32[32,1,128]{2,0,1:T(8,128)S(1)}, f32[32,1,128]{2,0,1:T(8,128)S(1)}, u32[]{:S(2)}, u32[]{:S(2)}) collective-permute-start(f32[32,1,128]{2,0,1:T(8,128)S(1)} %get-tuple-element.53), channel_id=1, source_target_pairs={{0,1},{1,4},{4,5},{5,8},{8,9},{9,12},{12,13},{2,3},{3,6},{6,7},{7,... | collective-permute-start | bytes 49160 | tf_op jit(solution)/shard_map/ppermute | solution.py:20
  4.8 5.3 %collective-permute-start.1 = (f32[32,1,128]{2,0,1:T(8,128)S(1)}, f32[32,1,128]{2,0,1:T(8,128)S(1)}, u32[]{:S(2)}, u32[]{:S(2)}) collective-permute-start(f32[32,1,128]{2,0,1:T(8,128)S(1)} %get-tuple-element.54), channel_id=1, source_target_pairs={{1,0},{4,1},{5,4},{8,5},{9,8},{12,9},{13,12},{3,2},{6,3},{7,6},{10... | collective-permute-start | bytes 49160 | tf_op jit(solution)/shard_map/ppermute | solution.py:21
  10.3 10.2 %collective-permute-start.2 = (f32[32,18,1]{2,0,1:T(8,128)S(1)}, f32[32,18,1]{2,0,1:T(8,128)S(1)}, u32[]{:S(2)}, u32[]{:S(2)}) collective-permute-start(f32[32,18,1]{2,0,1:T(8,128)S(1)} %get-tuple-element.42), channel_id=1, source_target_pairs={{2,0},{3,1},{6,4},{7,5},{10,8},{11,9},{14,12},{15,13},{18,16},{19,... | collective-permute-start | bytes 6920 | tf_op jit(solution)/shard_map/ppermute | solution.py:21
  11.6 10.7 %collective-permute-start.3 = (f32[32,18,1]{2,0,1:T(8,128)S(1)}, f32[32,18,1]{2,0,1:T(8,128)S(1)}, u32[]{:S(2)}, u32[]{:S(2)}) collective-permute-start(f32[32,18,1]{2,0,1:T(8,128)S(1)} %get-tuple-element.41), channel_id=1, source_target_pairs={{0,2},{1,3},{4,6},{5,7},{8,10},{9,11},{12,14},{13,15},{16,18},{17,... | collective-permute-start | bytes 6920 | tf_op jit(solution)/shard_map/ppermute | solution.py:20
  22.9 4.6 %collective-permute-start.4 = (f32[32,1,128]{2,0,1:T(8,128)S(1)}, f32[32,1,128]{2,0,1:T(8,128)S(1)}, u32[]{:S(2)}, u32[]{:S(2)}) collective-permute-start(f32[32,1,128]{2,0,1:T(8,128)S(1)} %get-tuple-element.51), channel_id=1, source_target_pairs={{0,1},{1,4},{4,5},{5,8},{8,9},{9,12},{12,13},{2,3},{3,6},{6,7},{7,... | collective-permute-start | bytes 49160 | tf_op jit(solution)/shard_map/ppermute | solution.py:20
  26.2 4.6 %collective-permute-start.5 = (f32[32,1,128]{2,0,1:T(8,128)S(1)}, f32[32,1,128]{2,0,1:T(8,128)S(1)}, u32[]{:S(2)}, u32[]{:S(2)}) collective-permute-start(f32[32,1,128]{2,0,1:T(8,128)S(1)} %get-tuple-element.52), channel_id=1, source_target_pairs={{1,0},{4,1},{5,4},{8,5},{9,8},{12,9},{13,12},{3,2},{6,3},{7,6},{10... | collective-permute-start | bytes 49160 | tf_op jit(solution)/shard_map/ppermute | solution.py:21
  31.0 10.1 %collective-permute-start.6 = (f32[32,18,1]{2,0,1:T(8,128)S(1)}, f32[32,18,1]{2,0,1:T(8,128)S(1)}, u32[]{:S(2)}, u32[]{:S(2)}) collective-permute-start(f32[32,18,1]{2,0,1:T(8,128)S(1)} %get-tuple-element.38), channel_id=1, source_target_pairs={{2,0},{3,1},{6,4},{7,5},{10,8},{11,9},{14,12},{15,13},{18,16},{19,... | collective-permute-start | bytes 6920 | tf_op jit(solution)/shard_map/ppermute | solution.py:21
  32.3 10.6 %collective-permute-start.7 = (f32[32,18,1]{2,0,1:T(8,128)S(1)}, f32[32,18,1]{2,0,1:T(8,128)S(1)}, u32[]{:S(2)}, u32[]{:S(2)}) collective-permute-start(f32[32,18,1]{2,0,1:T(8,128)S(1)} %get-tuple-element.37), channel_id=1, source_target_pairs={{0,2},{1,3},{4,6},{5,7},{8,10},{9,11},{12,14},{13,15},{16,18},{17,... | collective-permute-start | bytes 6920 | tf_op jit(solution)/shard_map/ppermute | solution.py:20
  43.6 4.7 %collective-permute-start.8 = (f32[32,1,128]{2,0,1:T(8,128)S(1)}, f32[32,1,128]{2,0,1:T(8,128)S(1)}, u32[]{:S(2)}, u32[]{:S(2)}) collective-permute-start(f32[32,1,128]{2,0,1:T(8,128)S(1)} %get-tuple-element.49), channel_id=1, source_target_pairs={{0,1},{1,4},{4,5},{5,8},{8,9},{9,12},{12,13},{2,3},{3,6},{6,7},{7,... | collective-permute-start | bytes 49160 | tf_op jit(solution)/shard_map/ppermute | solution.py:20
  47.0 4.5 %collective-permute-start.9 = (f32[32,1,128]{2,0,1:T(8,128)S(1)}, f32[32,1,128]{2,0,1:T(8,128)S(1)}, u32[]{:S(2)}, u32[]{:S(2)}) collective-permute-start(f32[32,1,128]{2,0,1:T(8,128)S(1)} %get-tuple-element.50), channel_id=1, source_target_pairs={{1,0},{4,1},{5,4},{8,5},{9,8},{12,9},{13,12},{3,2},{6,3},{7,6},{10... | collective-permute-start | bytes 49160 | tf_op jit(solution)/shard_map/ppermute | solution.py:21
  51.7 10.1 %collective-permute-start.10 = (f32[32,18,1]{2,0,1:T(8,128)S(1)}, f32[32,18,1]{2,0,1:T(8,128)S(1)}, u32[]{:S(2)}, u32[]{:S(2)}) collective-permute-start(f32[32,18,1]{2,0,1:T(8,128)S(1)} %get-tuple-element.34), channel_id=1, source_target_pairs={{2,0},{3,1},{6,4},{7,5},{10,8},{11,9},{14,12},{15,13},{18,16},{19,... | collective-permute-start | bytes 6920 | tf_op jit(solution)/shard_map/ppermute | solution.py:21
  53.0 10.6 %collective-permute-start.11 = (f32[32,18,1]{2,0,1:T(8,128)S(1)}, f32[32,18,1]{2,0,1:T(8,128)S(1)}, u32[]{:S(2)}, u32[]{:S(2)}) collective-permute-start(f32[32,18,1]{2,0,1:T(8,128)S(1)} %get-tuple-element.33), channel_id=1, source_target_pairs={{0,2},{1,3},{4,6},{5,7},{8,10},{9,11},{12,14},{13,15},{16,18},{17,... | collective-permute-start | bytes 6920 | tf_op jit(solution)/shard_map/ppermute | solution.py:20
  64.2 4.7 %collective-permute-start.12 = (f32[32,1,128]{2,0,1:T(8,128)S(1)}, f32[32,1,128]{2,0,1:T(8,128)S(1)}, u32[]{:S(2)}, u32[]{:S(2)}) collective-permute-start(f32[32,1,128]{2,0,1:T(8,128)S(1)} %get-tuple-element.47), channel_id=1, source_target_pairs={{0,1},{1,4},{4,5},{5,8},{8,9},{9,12},{12,13},{2,3},{3,6},{6,7},{7,... | collective-permute-start | bytes 49160 | tf_op jit(solution)/shard_map/ppermute | solution.py:20
  67.7 4.8 %collective-permute-start.13 = (f32[32,1,128]{2,0,1:T(8,128)S(1)}, f32[32,1,128]{2,0,1:T(8,128)S(1)}, u32[]{:S(2)}, u32[]{:S(2)}) collective-permute-start(f32[32,1,128]{2,0,1:T(8,128)S(1)} %get-tuple-element.48), channel_id=1, source_target_pairs={{1,0},{4,1},{5,4},{8,5},{9,8},{12,9},{13,12},{3,2},{6,3},{7,6},{10... | collective-permute-start | bytes 49160 | tf_op jit(solution)/shard_map/ppermute | solution.py:21
  72.6 10.1 %collective-permute-start.14 = (f32[32,18,1]{2,0,1:T(8,128)S(1)}, f32[32,18,1]{2,0,1:T(8,128)S(1)}, u32[]{:S(2)}, u32[]{:S(2)}) collective-permute-start(f32[32,18,1]{2,0,1:T(8,128)S(1)} %get-tuple-element.30), channel_id=1, source_target_pairs={{2,0},{3,1},{6,4},{7,5},{10,8},{11,9},{14,12},{15,13},{18,16},{19,... | collective-permute-start | bytes 6920 | tf_op jit(solution)/shard_map/ppermute | solution.py:21
  73.9 10.6 %collective-permute-start.15 = (f32[32,18,1]{2,0,1:T(8,128)S(1)}, f32[32,18,1]{2,0,1:T(8,128)S(1)}, u32[]{:S(2)}, u32[]{:S(2)}) collective-permute-start(f32[32,18,1]{2,0,1:T(8,128)S(1)} %get-tuple-element.29), channel_id=1, source_target_pairs={{0,2},{1,3},{4,6},{5,7},{8,10},{9,11},{12,14},{13,15},{16,18},{17,... | collective-permute-start | bytes 6920 | tf_op jit(solution)/shard_map/ppermute | solution.py:20
  85.1 4.7 %collective-permute-start.16 = (f32[32,1,128]{2,0,1:T(8,128)S(1)}, f32[32,1,128]{2,0,1:T(8,128)S(1)}, u32[]{:S(2)}, u32[]{:S(2)}) collective-permute-start(f32[32,1,128]{2,0,1:T(8,128)S(1)} %get-tuple-element.45), channel_id=1, source_target_pairs={{0,1},{1,4},{4,5},{5,8},{8,9},{9,12},{12,13},{2,3},{3,6},{6,7},{7,... | collective-permute-start | bytes 49160 | tf_op jit(solution)/shard_map/ppermute | solution.py:20
  88.6 4.0 %collective-permute-start.17 = (f32[32,1,128]{2,0,1:T(8,128)S(1)}, f32[32,1,128]{2,0,1:T(8,128)S(1)}, u32[]{:S(2)}, u32[]{:S(2)}) collective-permute-start(f32[32,1,128]{2,0,1:T(8,128)S(1)} %get-tuple-element.46), channel_id=1, source_target_pairs={{1,0},{4,1},{5,4},{8,5},{9,8},{12,9},{13,12},{3,2},{6,3},{7,6},{10... | collective-permute-start | bytes 49160 | tf_op jit(solution)/shard_map/ppermute | solution.py:21
  92.8 10.1 %collective-permute-start.18 = (f32[32,18,1]{2,0,1:T(8,128)S(1)}, f32[32,18,1]{2,0,1:T(8,128)S(1)}, u32[]{:S(2)}, u32[]{:S(2)}) collective-permute-start(f32[32,18,1]{2,0,1:T(8,128)S(1)} %get-tuple-element.26), channel_id=1, source_target_pairs={{2,0},{3,1},{6,4},{7,5},{10,8},{11,9},{14,12},{15,13},{18,16},{19,... | collective-permute-start | bytes 6920 | tf_op jit(solution)/shard_map/ppermute | solution.py:21
  94.1 10.6 %collective-permute-start.19 = (f32[32,18,1]{2,0,1:T(8,128)S(1)}, f32[32,18,1]{2,0,1:T(8,128)S(1)}, u32[]{:S(2)}, u32[]{:S(2)}) collective-permute-start(f32[32,18,1]{2,0,1:T(8,128)S(1)} %get-tuple-element.25), channel_id=1, source_target_pairs={{0,2},{1,3},{4,6},{5,7},{8,10},{9,11},{12,14},{13,15},{16,18},{17,... | collective-permute-start | bytes 6920 | tf_op jit(solution)/shard_map/ppermute | solution.py:20
  105.3 4.7 %collective-permute-start.20 = (f32[32,1,128]{2,0,1:T(8,128)S(1)}, f32[32,1,128]{2,0,1:T(8,128)S(1)}, u32[]{:S(2)}, u32[]{:S(2)}) collective-permute-start(f32[32,1,128]{2,0,1:T(8,128)S(1)} %get-tuple-element.43), channel_id=1, source_target_pairs={{0,1},{1,4},{4,5},{5,8},{8,9},{9,12},{12,13},{2,3},{3,6},{6,7},{7,... | collective-permute-start | bytes 49160 | tf_op jit(solution)/shard_map/ppermute | solution.py:20
  108.7 3.1 %collective-permute-start.21 = (f32[32,1,128]{2,0,1:T(8,128)S(1)}, f32[32,1,128]{2,0,1:T(8,128)S(1)}, u32[]{:S(2)}, u32[]{:S(2)}) collective-permute-start(f32[32,1,128]{2,0,1:T(8,128)S(1)} %get-tuple-element.44), channel_id=1, source_target_pairs={{1,0},{4,1},{5,4},{8,5},{9,8},{12,9},{13,12},{3,2},{6,3},{7,6},{10... | collective-permute-start | bytes 49160 | tf_op jit(solution)/shard_map/ppermute | solution.py:21
  112.0 10.1 %collective-permute-start.22 = (f32[32,18,1]{2,0,1:T(8,128)S(1)}, f32[32,18,1]{2,0,1:T(8,128)S(1)}, u32[]{:S(2)}, u32[]{:S(2)}) collective-permute-start(f32[32,18,1]{2,0,1:T(8,128)S(1)} %get-tuple-element.22), channel_id=1, source_target_pairs={{2,0},{3,1},{6,4},{7,5},{10,8},{11,9},{14,12},{15,13},{18,16},{19,... | collective-permute-start | bytes 6920 | tf_op jit(solution)/shard_map/ppermute | solution.py:21
  113.3 10.6 %collective-permute-start.23 = (f32[32,18,1]{2,0,1:T(8,128)S(1)}, f32[32,18,1]{2,0,1:T(8,128)S(1)}, u32[]{:S(2)}, u32[]{:S(2)}) collective-permute-start(f32[32,18,1]{2,0,1:T(8,128)S(1)} %get-tuple-element.21), channel_id=1, source_target_pairs={{0,2},{1,3},{4,6},{5,7},{8,10},{9,11},{12,14},{13,15},{16,18},{17,... | collective-permute-start | bytes 6920 | tf_op jit(solution)/shard_map/ppermute | solution.py:20
